TPU v7x, 32 devices: a whole 2x2x4 slice. The times are simulated.
32 devices in a mesh: row: 2 (over x), col: 16 (over z, y, core).
Axes of the slice: x: 2, y: 2, z: 4, core: 2. Of those that a mesh axis runs over, the one named last changes fastest.
Arguments:
- hessian_old: float32 [2048, 12288], P('row', 'col'), may hold values from -6 to 6
- gate_rows: bfloat16 [512, 2048], P('col', 'row'), may hold values from -9 to 9
- up_rows: bfloat16 [512, 2048], P('col', 'row'), may hold values from -15 to 15
- gate_columns: bfloat16 [512, 12288], P('row', 'col'), may hold values from -9 to 9
- up_columns: bfloat16 [512, 12288], P('row', 'col'), may hold values from -15 to 15
Outputs:
- hessian_new: float32 [2048, 12288], P('row', 'col')
All inputs are finite; a program needn't handle non-finite values.
Results may differ from a plain program's by a relative error of at most 0.00099.
Values may be sent and summed in bfloat16 or wider, within the bound.
A program may use at most 64 MiB of HBM per device.

v0:
```python
import jax
import jax.numpy as jnp
from jax import lax
from jax.sharding import PartitionSpec as P


def silu_product(gate, up):
    return (jax.nn.silu(gate.astype(jnp.float32)) * up.astype(jnp.float32)).astype(jnp.bfloat16)


def body(hessian_old, gate_rows, up_rows, gate_columns, up_columns):
    total_tokens = lax.axis_size("col") * gate_rows.shape[0]
    row_formed = silu_product(gate_rows, up_rows)
    column_formed = silu_product(gate_columns, up_columns)
    column_gathered = lax.all_gather(column_formed, "row", axis=0, tiled=True)
    product = lax.dot_general(
        lax.all_gather(row_formed, "col", axis=0, tiled=True),
        column_gathered,
        (((0,), (0,)), ((), ())),
        preferred_element_type=jnp.float32,
    )
    return 0.5 * hessian_old + product / total_tokens


def solution(mesh):
    in_specs = (P("row", "col"), P("col", "row"), P("col", "row"), P("row", "col"), P("row", "col"))
    out_specs = P("row", "col")
    return jax.shard_map(body, mesh=mesh, in_specs=in_specs, out_specs=out_specs, check_vma=False)
```

profile of v0, /device:TPU:0, one launch (start us, length us, event | category | flops | bytes accessed | tf_op | source)
XLA Modules:
  0.0 61.9 jit_solution(4926446980811626307)
XLA Ops:
  6.5 0.0 all-gather.2.cloned.1.call-start
  6.5 1.5 %fusion.9 = bf16[32,1024]{1,0:T(8,128)(2,1)} fusion(bf16[32,1024]{1,0:T(8,128)(2,1)} %param.7, bf16[32,1024]{1,0:T(8,128)(2,1)} %param.6), kind=kLoop, calls=%fused_computation.14 | loop fusion | flops 262144 | bytes 196608 | tf_op jit(solution)/shard_map/convert_element_type | solution.py:8
  8.1 0.0 all-gather.2.cloned.1.call-update
  8.1 1.4 %fusion.4 = bf16[256,768]{1,0:T(8,128)(2,1)S(1)} fusion(bf16[256,768]{1,0:T(8,128)(2,1)} %param.9, bf16[256,768]{1,0:T(8,128)(2,1)} %param.8), kind=kLoop, calls=%fused_computation.7 | loop fusion | flops 1572864 | bytes 1179648 | tf_op jit(solution)/shard_map/convert_element_type | solution.py:8
  9.5 12.8 %all_gather.7 = bf16[512,768]{1,0:T(8,128)(2,1)S(1)} all-gather(bf16[256,768]{1,0:T(8,128)(2,1)S(1)} %fusion.4), channel_id=1, replica_groups=mesh['row'=2,'col'=16] {'row'}, dimensions={0}, use_global_device_ids=true | all-gather | bytes 1179648 | tf_op jit(solution)/shard_map/all_gather | solution.py:15
  22.2 27.9 %all-gather.2.cloned.1.call-done = bf16[512,1024]{1,0:T(8,128)(2,1)} async-done(((bf16[32,1024]{1,0:T(8,128)(2,1)}), bf16[512,1024]{1,0:T(8,128)(2,1)}) %all-gather.2.cloned.1.call-update) | async-done | bytes 1048592 | tf_op jit(solution)/shard_map/all_gather | solution.py:17
  50.1 4.9 %multiply_add_fusion = f32[1024,768]{1,0:T(8,128)} fusion(f32[1024,768]{1,0:T(8,128)} %param.5, bf16[512,1024]{1,0:T(8,128)(2,1)} %all-gather.2.cloned.1.call-done, bf16[512,768]{1,0:T(8,128)(2,1)S(1)} %all_gather.7), kind=kOutput, calls=%fused_computation | convolution fusion | flops 807665664 | bytes 8126464 | tf_op jit(solution)/shard_map/dot_general | solution.py:16
Async XLA Ops:
  6.5 43.6 %all-gather.2.cloned.1.call-start = ((), (), s32[]{:S(2)}) async-start(), calls=%async_computation | async-start | bytes 1114112 | tf_op jit(solution)/shard_map/all_gather | solution.py:17
Sparse Core Ops, SparseCore 0:
  9.5 40.5 all-gather.1
where the time goes:
time: 62.1 us; the launch traced here: 61.9 us
  waiting for transfers between devices  27.9 us (45%)
  between operations  13.4 us (22%)
  blocking collectives  12.8 us (21%)
  matrix products  4.9 us (8%)
  other arithmetic  2.92 us (5%)
    all_gather x1, waiting for transfers between devices, body(): lax.all_gather(row_formed, 'col', axis=0, tiled=True)  27.9 us
    all_gather x1, blocking collectives, body(): column_gathered = lax.all_gather(column_formed, 'row', axis=0, tiled=True)  12.8 us
    dot_general x1, matrix products, body(): lax.dot_general(lax.all_gather(row_formed, 'col', axis=0, tiled=True), co...  4.9 us
    convert_element_type x2, other arithmetic, silu_product(): (jax.nn.silu(gate.astype(jnp.float32)) * up.astype(jnp.float32)).astype(j...  2.92 us
  transfers between devices with their start and end apart: 1, of which 1 were waited for; matrix products, arithmetic and copies ran while one was open for 2% of the time, Pallas kernels for 0%

commit v1 on v0

--- a/solution.py
+++ b/solution.py
@@ -2,6 +2,27 @@
 import jax.numpy as jnp
 from jax import lax
 from jax.sharding import PartitionSpec as P
+
+
+def in_order(blocks, dim):
+    blocks = jnp.moveaxis(blocks, 0, dim)
+    lengths = blocks.shape
+    return blocks.reshape(*lengths[:dim], lengths[dim] * lengths[dim + 1], *lengths[dim + 2 :])
+
+
+def collected_by_bits(value, axis):
+    count, index = (lax.axis_size(axis), lax.axis_index(axis))
+    tiles, bit = (value[None], 1)
+    while bit < count:
+        other = lax.ppermute(tiles, axis, [(i, i ^ bit) for i in range(count)])
+        low = index & bit == 0
+        tiles = jnp.concatenate([jnp.where(low, tiles, other), jnp.where(low, other, tiles)])
+        bit *= 2
+    return tiles
+
+
+def collect(x, axis, dim):
+    return in_order(collected_by_bits(x, axis), dim)
 
 
 def silu_product(gate, up):
@@ -14,7 +35,7 @@
     column_formed = silu_product(gate_columns, up_columns)
     column_gathered = lax.all_gather(column_formed, "row", axis=0, tiled=True)
     product = lax.dot_general(
-        lax.all_gather(row_formed, "col", axis=0, tiled=True),
+        collect(row_formed, "col", 0),
         column_gathered,
         (((0,), (0,)), ((), ())),
         preferred_element_type=jnp.float32,

time: 62.1 us -> 45.1 us (0.73)
  between operations: 13.4 us -> 0.07 us
  starting transfers between devices: 0.01 us -> 7.94 us
  waiting for transfers between devices: 27.9 us -> 22.6 us
  blocking collectives: 12.8 us -> 9.98 us
  matrix products: 4.9 us -> 2.74 us
  other arithmetic: 2.92 us -> 1.58 us
    all_gather x1 -> x0, waiting for transfers between devices: 27.9 us -> none  [body(): lax.all_gather(row_formed, 'col', axis=0, tiled=True)]
    ppermute x0 -> x4, waiting for transfers between devices: none -> 22.6 us  [collected_by_bits(): other = lax.ppermute(tiles, axis, [(i, i ^ bit) for i in range(count)])]
    ppermute x0 -> x4, starting transfers between devices: none -> 7.94 us  [collected_by_bits(): other = lax.ppermute(tiles, axis, [(i, i ^ bit) for i in range(count)])]
    all_gather x1, blocking collectives: 12.8 us -> 9.98 us  [body(): column_gathered = lax.all_gather(column_formed, 'row', axis=0, tiled=True)]
    convert_element_type x2 -> x1, other arithmetic: 2.92 us -> 0.25 us  [silu_product(): (jax.nn.silu(gate.astype(jnp.float32)) * up.astype(jnp.float32)).astype(j...]
    dot_general x1, matrix products: 4.9 us -> 2.74 us  [body(): lax.dot_general(collect(row_formed, 'col', 0), column_gathered, (((0,), (...]
    broadcast_in_dim x0 -> x1, other arithmetic: none -> 0.99 us  [collected_by_bits(): tiles, bit = (value[None], 1)]
  transfers between devices with their start and end apart: 1 -> 4, of which waited for: 1 -> 4; matrix products, arithmetic and copies ran while one was open for 2% -> 1% of each run, Pallas kernels for 0% -> 0%
where the time goes in v1:
time: 45.1 us; the launch traced here: 44.9 us
  waiting for transfers between devices  22.6 us (50%)
  blocking collectives  9.98 us (22%)
  starting transfers between devices  7.94 us (18%)
  matrix products  2.74 us (6%)
  other arithmetic  1.58 us (4%)
    ppermute x4, waiting for transfers between devices, collected_by_bits(): other = lax.ppermute(tiles, axis, [(i, i ^ bit) for i in range(count)])  22.6 us
    all_gather x1, blocking collectives, body(): column_gathered = lax.all_gather(column_formed, 'row', axis=0, tiled=True)  9.98 us
    ppermute x4, starting transfers between devices, collected_by_bits(): other = lax.ppermute(tiles, axis, [(i, i ^ bit) for i in range(count)])  7.94 us
    dot_general x1, matrix products, body(): lax.dot_general(collect(row_formed, 'col', 0), column_gathered, (((0,), (...  2.74 us
    broadcast_in_dim x1, other arithmetic, collected_by_bits(): tiles, bit = (value[None], 1)  0.99 us
  transfers between devices with their start and end apart: 4, of which 4 were waited for; matrix products, arithmetic and copies ran while one was open for 1% of the time, Pallas kernels for 0%

profile of v1, /device:TPU:0, one launch (start us, length us, event | category | flops | bytes accessed | tf_op | source)
XLA Modules:
  0.0 44.9 jit_solution(648638336323696976)
XLA Ops:
  0.0 0.0 copy-start.1
  0.0 0.0 copy-start.2
  0.0 1.0 %fusion.10 = bf16[1,32,1024]{2,1,0:T(8,128)(2,1)S(1)} fusion(bf16[32,1024]{1,0:T(8,128)(2,1)} %param.7, bf16[32,1024]{1,0:T(8,128)(2,1)} %param.6), kind=kLoop, calls=%fused_computation.25 | loop fusion | flops 262144 | bytes 196608 | tf_op jit(solution)/shard_map/broadcast_in_dim | solution.py:15
  1.0 0.6 %collective-permute-start = (bf16[1,32,1024]{2,1,0:T(8,128)(2,1)S(1)}, bf16[1,32,1024]{2,1,0:T(8,128)(2,1)S(1)}, u32[]{:S(2)}, u32[]{:S(2)}) collective-permute-start(bf16[1,32,1024]{2,1,0:T(8,128)(2,1)S(1)} %fusion.10), channel_id=1, source_target_pairs={{0,1},{1,0},{2,3},{3,2},{4,5},{5,4},{6,7},{7,6},{8,9},{9,8},{10,11... | collective-permute-start | bytes 196616 | tf_op jit(solution)/shard_map/ppermute | solution.py:17
  1.6 0.9 %collective-permute-done = bf16[1,32,1024]{2,1,0:T(8,128)(2,1)S(1)} collective-permute-done((bf16[1,32,1024]{2,1,0:T(8,128)(2,1)S(1)}, bf16[1,32,1024]{2,1,0:T(8,128)(2,1)S(1)}, u32[]{:S(2)}, u32[]{:S(2)}) %collective-permute-start) | collective-permute-done | bytes 65568 | tf_op jit(solution)/shard_map/ppermute | solution.py:17
  2.5 2.9 %collective-permute-start.1 = (bf16[2,32,1024]{2,1,0:T(8,128)(2,1)S(1)}, bf16[2,32,1024]{2,1,0:T(8,128)(2,1)S(1)}, u32[]{:S(2)}, u32[]{:S(2)}) collective-permute-start(bf16[2,32,1024]{2,1,0:T(8,128)(2,1)S(1)} %pad_maximum_fusion.3), channel_id=1, source_target_pairs={{0,2},{1,3},{2,0},{3,1},{4,6},{5,7},{6,4},{7,5},{8,10},{9,11},{10,... | collective-permute-start | bytes 393224 | tf_op jit(solution)/shard_map/ppermute | solution.py:17
  5.4 3.8 %collective-permute-done.1 = bf16[2,32,1024]{2,1,0:T(8,128)(2,1)S(1)} collective-permute-done((bf16[2,32,1024]{2,1,0:T(8,128)(2,1)S(1)}, bf16[2,32,1024]{2,1,0:T(8,128)(2,1)S(1)}, u32[]{:S(2)}, u32[]{:S(2)}) %collective-permute-start.1) | collective-permute-done | bytes 131104 | tf_op jit(solution)/shard_map/ppermute | solution.py:17
  9.3 1.9 %collective-permute-start.2 = (bf16[4,32,1024]{2,1,0:T(8,128)(2,1)S(1)}, bf16[4,32,1024]{2,1,0:T(8,128)(2,1)S(1)}, u32[]{:S(2)}, u32[]{:S(2)}) collective-permute-start(bf16[4,32,1024]{2,1,0:T(8,128)(2,1)S(1)} %pad_maximum_fusion.2), channel_id=1, source_target_pairs={{0,4},{1,5},{2,6},{3,7},{4,0},{5,1},{6,2},{7,3},{8,12},{9,13},{10,... | collective-permute-start | bytes 786440 | tf_op jit(solution)/shard_map/ppermute | solution.py:17
  11.2 6.0 %collective-permute-done.2 = bf16[4,32,1024]{2,1,0:T(8,128)(2,1)S(1)} collective-permute-done((bf16[4,32,1024]{2,1,0:T(8,128)(2,1)S(1)}, bf16[4,32,1024]{2,1,0:T(8,128)(2,1)S(1)}, u32[]{:S(2)}, u32[]{:S(2)}) %collective-permute-start.2) | collective-permute-done | bytes 262176 | tf_op jit(solution)/shard_map/ppermute | solution.py:17
  17.3 2.6 %collective-permute-start.3 = (bf16[8,32,1024]{2,1,0:T(8,128)(2,1)S(1)}, bf16[8,32,1024]{2,1,0:T(8,128)(2,1)S(1)}, u32[]{:S(2)}, u32[]{:S(2)}) collective-permute-start(bf16[8,32,1024]{2,1,0:T(8,128)(2,1)S(1)} %pad_maximum_fusion.1), channel_id=1, source_target_pairs={{0,8},{1,9},{2,10},{3,11},{4,12},{5,13},{6,14},{7,15},{8,0},{9,1},... | collective-permute-start | bytes 1572872 | tf_op jit(solution)/shard_map/ppermute | solution.py:17
  19.9 0.0 copy-done.1
  19.9 0.0 copy-done.2
  19.9 0.0 copy-start
  19.9 0.3 fusion.4
  20.1 10.0 %all_gather.3 = bf16[512,768]{1,0:T(8,128)(2,1)S(1)} all-gather(bf16[256,768]{1,0:T(8,128)(2,1)S(1)} %fusion.4), channel_id=1, replica_groups=mesh['row'=2,'col'=16] {'row'}, dimensions={0}, use_global_device_ids=true | all-gather | bytes 1179648 | tf_op jit(solution)/shard_map/all_gather | solution.py:36
  30.1 11.9 %collective-permute-done.3 = bf16[8,32,1024]{2,1,0:T(8,128)(2,1)S(1)} collective-permute-done((bf16[8,32,1024]{2,1,0:T(8,128)(2,1)S(1)}, bf16[8,32,1024]{2,1,0:T(8,128)(2,1)S(1)}, u32[]{:S(2)}, u32[]{:S(2)}) %collective-permute-start.3) | collective-permute-done | bytes 524320 | tf_op jit(solution)/shard_map/ppermute | solution.py:17
  42.0 0.1 broadcast_select_fusion.1
  42.1 0.1 pad_maximum_fusion
  42.2 0.0 copy-done
  42.2 2.7 %multiply_add_fusion = f32[1024,768]{1,0:T(8,128)} fusion(f32[1024,768]{1,0:T(8,128)S(1)} %copy-done, bf16[512,1024]{1,0:T(8,128)(2,1)S(1)} %bitcast.5, bf16[512,768]{1,0:T(8,128)(2,1)S(1)} %all_gather.3), kind=kOutput, calls=%fused_computation | convolution fusion | flops 807665664 | bytes 8126464 | tf_op jit(solution)/shard_map/dot_general | solution.py:37
  (6 shorter events, 0.2 us)
Async XLA Ops:
  0.0 19.9 %copy-start.1 = (bf16[256,768]{1,0:T(8,128)(2,1)S(1)}, bf16[256,768]{1,0:T(8,128)(2,1)}, u32[]{:S(2)}) copy-start(bf16[256,768]{1,0:T(8,128)(2,1)} %param.9) | copy-start | bytes 1179652
  0.0 19.9 %copy-start.2 = (bf16[256,768]{1,0:T(8,128)(2,1)S(1)}, bf16[256,768]{1,0:T(8,128)(2,1)}, u32[]{:S(2)}) copy-start(bf16[256,768]{1,0:T(8,128)(2,1)} %param.8) | copy-start | bytes 1179652
  1.0 1.5 %collective-permute-start = (bf16[1,32,1024]{2,1,0:T(8,128)(2,1)S(1)}, bf16[1,32,1024]{2,1,0:T(8,128)(2,1)S(1)}, u32[]{:S(2)}, u32[]{:S(2)}) collective-permute-start(bf16[1,32,1024]{2,1,0:T(8,128)(2,1)S(1)} %fusion.10), channel_id=1, source_target_pairs={{0,1},{1,0},{2,3},{3,2},{4,5},{5,4},{6,7},{7,6},{8,9},{9,8},{10,11... | collective-permute-start | bytes 196616 | tf_op jit(solution)/shard_map/ppermute | solution.py:17
  2.5 6.7 %collective-permute-start.1 = (bf16[2,32,1024]{2,1,0:T(8,128)(2,1)S(1)}, bf16[2,32,1024]{2,1,0:T(8,128)(2,1)S(1)}, u32[]{:S(2)}, u32[]{:S(2)}) collective-permute-start(bf16[2,32,1024]{2,1,0:T(8,128)(2,1)S(1)} %pad_maximum_fusion.3), channel_id=1, source_target_pairs={{0,2},{1,3},{2,0},{3,1},{4,6},{5,7},{6,4},{7,5},{8,10},{9,11},{10,... | collective-permute-start | bytes 393224 | tf_op jit(solution)/shard_map/ppermute | solution.py:17
  9.3 7.9 %collective-permute-start.2 = (bf16[4,32,1024]{2,1,0:T(8,128)(2,1)S(1)}, bf16[4,32,1024]{2,1,0:T(8,128)(2,1)S(1)}, u32[]{:S(2)}, u32[]{:S(2)}) collective-permute-start(bf16[4,32,1024]{2,1,0:T(8,128)(2,1)S(1)} %pad_maximum_fusion.2), channel_id=1, source_target_pairs={{0,4},{1,5},{2,6},{3,7},{4,0},{5,1},{6,2},{7,3},{8,12},{9,13},{10,... | collective-permute-start | bytes 786440 | tf_op jit(solution)/shard_map/ppermute | solution.py:17
  17.3 24.8 %collective-permute-start.3 = (bf16[8,32,1024]{2,1,0:T(8,128)(2,1)S(1)}, bf16[8,32,1024]{2,1,0:T(8,128)(2,1)S(1)}, u32[]{:S(2)}, u32[]{:S(2)}) collective-permute-start(bf16[8,32,1024]{2,1,0:T(8,128)(2,1)S(1)} %pad_maximum_fusion.1), channel_id=1, source_target_pairs={{0,8},{1,9},{2,10},{3,11},{4,12},{5,13},{6,14},{7,15},{8,0},{9,1},... | collective-permute-start | bytes 1572872 | tf_op jit(solution)/shard_map/ppermute | solution.py:17
  19.9 22.3 %copy-start = (f32[1024,768]{1,0:T(8,128)S(1)}, f32[1024,768]{1,0:T(8,128)}, u32[]{:S(2)}) copy-start(f32[1024,768]{1,0:T(8,128)} %param.5) | copy-start | bytes 9437188
